TPU v7x, 512 devices: a whole 4x8x8 slice. The times are simulated.
512 devices in a mesh: dp: 16 (over y, core), ctx: 32 (over z, x).
Axes of the slice: x: 4, y: 8, z: 8, core: 2. Of those that a mesh axis runs over, the one named last changes fastest.
Arguments:
- delta_query_rows: bfloat16 [16, 4096, 16, 128], P('dp', 'ctx'), may hold values from -6 to 6
- delta_key_rows: bfloat16 [16, 4096, 16, 128], P('dp', 'ctx'), may hold values from -6 to 6
- delta_value_rows: bfloat16 [16, 4096, 16, 128], P('dp', 'ctx'), may hold values from -6 to 6
- delta_write_strength: float32 [16, 4096, 16], P('dp', 'ctx'), may hold values from 0.2 to 1
- token_gate_scale: float32 [16, 4096, 16], P('dp', 'ctx'), may hold values from 0.5 to 2
- channel_decay_rate: float32 [16, 128], replicated, may hold values from 0.00390625 to 0.0625
- sudden_loss_mask: int32 [16, 4096], P('dp', 'ctx'), may hold values 0 or 1
- document_numbers: int32 [16, 4096], P('dp'), may hold values from 0 to 63, never falling along the last dimension, each value on 1 to 128 neighbouring positions
- delta_norm_gain: float32 [128], replicated, may hold values from 0.5 to 1.5
- delta_output_cotangent: bfloat16 [16, 4096, 16, 128], P('dp', 'ctx'), may hold values from -6 to 6
- latent_query_rows: bfloat16 [16, 4096, 16, 128], P('dp', 'ctx'), may hold values from -90 to 90
- compressed_latents: bfloat16 [16, 4096, 512], P('dp', 'ctx'), may hold values from -90 to 90
- query_to_latent_map: bfloat16 [16, 128, 512], P(None, 'ctx'), may hold values from -0.5 to 0.5
- latent_to_value_map: bfloat16 [16, 512, 128], P(None, 'ctx'), may hold values from -0.25 to 0.25
Outputs:
- kda_output: bfloat16 [16, 4096, 16, 128], P('dp', 'ctx')
- mla_output: bfloat16 [16, 4096, 16, 128], P('dp', 'ctx')
- gain_grad: float32 [128], replicated
Inputs may be any that keep to these rules, and one draw needn't show every extreme that they name: `document_numbers`: each row's document numbers never fall; every document has 1 to 128 tokens, and some document has exactly 128.
All inputs are finite; a program needn't handle non-finite values. No bound on the sum of `sudden_loss_mask` on one device may be relied on, other than what follows from the above.
Results may differ from a plain program's by a relative error of at most 0.0065.
The roundings to bfloat16 on the way count: a program that leaves them out, or rounds other values in their place, can miss the bound.
Values may be sent and summed in bfloat16 or wider, within the bound.
No kernel may reach another device: no remote copies, remote signals or barrier semaphores. Data moves between devices by JAX's collectives and lax.ppermute only.
A program may use at most 128 MiB of HBM per device.

v0:
```python
import math
import jax
import jax.numpy as jnp
from jax import lax
from jax.sharding import PartitionSpec as P

DOCBLK = 2
DN = 128
exact_mode = lax.Precision.HIGHEST


def from_behind(value, axis, steps):
    count = lax.axis_size(axis)
    leading, last = (max(0, -steps), min(count, count - steps))
    return lax.ppermute(value, axis, [(source, source + steps) for source in range(leading, last)])


def unit_norm(tensor):
    widened = tensor.astype(jnp.float32)
    return widened * lax.rsqrt(jnp.sum(widened * widened, axis=-1, keepdims=True) + 1e-06)


def block_maps(queries, keyset, values, writes, log_decay_values, docs, before):
    size = docs.shape[0]
    places = jnp.arange(size, dtype=jnp.int32)
    same_doc = docs[:, None] == docs[None, :]
    within = (same_doc & (places[:, None] >= places[None, :])).astype(jnp.float32)
    earlier = (same_doc & (places[:, None] > places[None, :])).astype(jnp.float32)
    cumlog = jnp.einsum("ts,shc->thc", within, log_decay_values, precision=exact_mode)
    key_decayed = keyset * jnp.exp(cumlog)
    key_grown = keyset * jnp.exp(-cumlog)
    query_decayed = queries * jnp.exp(cumlog)
    carried = (docs == before).astype(jnp.float32)
    pairwise = jnp.einsum("thc,shc->hts", key_decayed, key_grown, precision=exact_mode)
    triangle = pairwise * jnp.transpose(writes)[:, :, None] * earlier[None]
    targets = jnp.concatenate(
        [writes[:, :, None] * values, (writes * carried[:, None])[:, :, None] * key_decayed],
        axis=-1,
    )
    identity_mat = jnp.eye(size, dtype=jnp.float32)
    solved = jax.scipy.linalg.solve_triangular(
        identity_mat[None] + triangle,
        jnp.transpose(targets, (1, 0, 2)),
        lower=True,
        unit_diagonal=True,
    )
    value_width = values.shape[-1]
    from_values = solved[:, :, :value_width]
    from_state = solved[:, :, value_width:]
    weights_att = (
        jnp.einsum("thc,shc->hts", query_decayed, key_grown, precision=exact_mode) * within[None]
    )
    local_out = jnp.einsum("hts,hsv->thv", weights_att, from_values, precision=exact_mode)
    state_query = carried[:, None, None] * query_decayed - jnp.einsum(
        "hts,hsc->thc", weights_att, from_state, precision=exact_mode
    )
    closing = jnp.exp(cumlog[size - 1])
    tailing = (docs == docs[size - 1]).astype(jnp.float32)
    leaving = key_grown * closing[None] * tailing[:, None, None]
    key_width = keyset.shape[-1]
    transfer_map = (carried[size - 1] * closing)[:, :, None] * jnp.eye(
        key_width, dtype=jnp.float32
    )[None]
    transfer_map = transfer_map - jnp.einsum(
        "shc,hsd->hcd", leaving, from_state, precision=exact_mode
    )
    offset_map = jnp.einsum("shc,hsv->hcv", leaving, from_values, precision=exact_mode)
    return (local_out, state_query, transfer_map, offset_map)


def advance(transfer_map, offset_map, state):
    return jnp.einsum("shcd,shdv->shcv", transfer_map, state, precision=exact_mode) + offset_map


def shards(
    delta_query_rows,
    delta_key_rows,
    delta_value_rows,
    delta_write_strength,
    token_gate_scale,
    channel_decay_rate,
    sudden_loss_mask,
    document_numbers,
    delta_norm_gain,
    delta_output_cotangent,
    latent_query_rows,
    compressed_latents,
    query_to_latent_map,
    latent_to_value_map,
):
    ranks = lax.axis_size("ctx")
    place = lax.axis_index("ctx")
    seqs = delta_query_rows.shape[0]
    rows = delta_query_rows.shape[1]
    half = rows // 2
    heads = delta_query_rows.shape[2]
    key_width = delta_query_rows.shape[3]
    value_width = delta_value_rows.shape[3]
    second_block = 2 * ranks - 1 - place
    zero_index = jnp.zeros((), jnp.int32)

    def block_docs(block):
        start = block * half
        docs = lax.dynamic_slice_in_dim(document_numbers, start, half, 1)
        prior = lax.dynamic_slice_in_dim(document_numbers, jnp.maximum(start - 1, 0), 1, 1)[:, 0]
        return (docs, jnp.where(block > 0, prior, -1))

    docs_first, prior_first = block_docs(place)
    docs_second, prior_second = block_docs(second_block)
    docs_pair = jnp.stack([docs_first, docs_second], axis=1)
    prior_pair = jnp.stack([prior_first, prior_second], axis=1)

    def split_rows(tensor):
        return tensor.reshape((seqs, 2, half) + tensor.shape[2:])

    queries = split_rows(unit_norm(delta_query_rows))
    keyset = split_rows(unit_norm(delta_key_rows))
    values = split_rows(delta_value_rows.astype(jnp.float32))
    writes = split_rows(delta_write_strength)
    log_decay_values = split_rows(
        -channel_decay_rate[None, None] * token_gate_scale[..., None]
        + sudden_loss_mask.astype(jnp.float32)[:, :, None, None] * math.log(0.6)
    )
    local_out, state_query, transfer_map, offset_map = jax.vmap(jax.vmap(block_maps))(
        queries, keyset, values, writes, log_decay_values, docs_pair, prior_pair
    )
    zero_state = jnp.zeros((seqs, heads, key_width, value_width), jnp.float32)
    state_first = zero_state
    state_second = zero_state
    for repeat in range(DOCBLK):
        out_first = advance(transfer_map[:, 0], offset_map[:, 0], state_first)
        out_second = advance(transfer_map[:, 1], offset_map[:, 1], state_second)
        state_first = from_behind(out_first, "ctx", 1)
        from_above = from_behind(out_second, "ctx", -1)
        state_second = jnp.where(place == ranks - 1, out_first, from_above)
    states = jnp.stack([state_first, state_second], axis=1)
    kda_raw = local_out + jnp.einsum(
        "sbthc,sbhcv->sbthv", state_query, states, precision=exact_mode
    )
    kda_raw = kda_raw.reshape(seqs, rows, heads, value_width)
    meansq = jnp.mean(kda_raw * kda_raw, axis=-1, keepdims=True)
    normed = kda_raw * lax.rsqrt(meansq + 1e-06)
    kda_output = (normed * delta_norm_gain).astype(jnp.bfloat16)
    partial_grad = jnp.sum(normed * delta_output_cotangent.astype(jnp.float32), axis=(0, 1, 2))
    total_grad = lax.psum(partial_grad, ("dp", "ctx"))
    gain_grad = total_grad / math.sqrt(seqs * lax.axis_size("dp") * rows * ranks * heads)
    latent_width = compressed_latents.shape[2]
    neighbours = {0: compressed_latents}
    offsets = []
    for distance in range(1, DOCBLK + 1):
        offsets.append(distance)
        offsets.append(-distance)
    for offset in offsets:
        neighbours[offset] = from_behind(compressed_latents, "ctx", offset)
    stacked = jnp.stack([neighbours[offset] for offset in range(-DOCBLK, DOCBLK + 1)], axis=0)
    stacked = stacked.reshape(2 * DOCBLK + 1, seqs, 2, half, latent_width)
    lift_keys, lift_values = (
        lax.all_gather(query_to_latent_map, "ctx", axis=1, tiled=True),
        lax.all_gather(latent_to_value_map, "ctx", axis=1, tiled=True),
    )
    lifted = jnp.einsum(
        "sthn,hnl->sthl", latent_query_rows, lift_keys, preferred_element_type=jnp.float32
    ).astype(jnp.bfloat16)
    scale = 1.0 / math.sqrt(DN)
    halves_out = []
    for which in range(2):
        block = place if which == 0 else second_block
        key_parts = []
        doc_parts = []
        pos_parts = []
        for back in range(DOCBLK, -1, -1):
            source = block - back
            in_first = source < ranks
            owner = jnp.where(in_first, source, 2 * ranks - 1 - source)
            side = jnp.where(in_first, 0, 1).astype(jnp.int32)
            slot = jnp.clip(place - owner, -DOCBLK, DOCBLK) + DOCBLK
            piece = lax.dynamic_slice(
                stacked,
                (slot, zero_index, side, zero_index, zero_index),
                (1, seqs, 1, half, latent_width),
            )
            key_parts.append(piece.reshape(seqs, half, latent_width))
            source_docs = lax.dynamic_slice_in_dim(
                document_numbers, jnp.maximum(source, 0) * half, half, 1
            )
            doc_parts.append(jnp.where(source >= 0, source_docs, -1))
            pos_parts.append(source * half + jnp.arange(half, dtype=jnp.int32))
        key_rows = jnp.concatenate(key_parts, axis=1)
        key_docs = jnp.concatenate(doc_parts, axis=1)
        key_pos = jnp.concatenate(pos_parts, axis=0)
        query_docs = docs_pair[:, which]
        query_pos = block * half + jnp.arange(half, dtype=jnp.int32)
        block_query = lifted[:, which * half : (which + 1) * half]
        logits = (
            jnp.einsum("sthl,skl->shtk", block_query, key_rows, preferred_element_type=jnp.float32)
            * scale
        )
        allowed = (query_docs[:, None, :, None] == key_docs[:, None, None, :]) & (
            key_pos[None, None, None, :] <= query_pos[None, None, :, None]
        )
        logits = jnp.where(allowed, logits, -jnp.inf)
        peak = jnp.max(logits, axis=-1, keepdims=True)
        expo = jnp.exp(logits - peak)
        probs = (expo / jnp.sum(expo, axis=-1, keepdims=True)).astype(jnp.bfloat16)
        latent_mix = jnp.einsum(
            "shtk,skl->sthl", probs, key_rows, preferred_element_type=jnp.float32
        ).astype(jnp.bfloat16)
        halves_out.append(
            jnp.einsum(
                "sthl,hlv->sthv", latent_mix, lift_values, preferred_element_type=jnp.float32
            ).astype(jnp.bfloat16)
        )
    mla_output = jnp.concatenate(halves_out, axis=1)
    return (kda_output, mla_output, gain_grad)


def solution(mesh):
    placed = (
        P("dp", "ctx", None, None),
        P("dp", "ctx", None, None),
        P("dp", "ctx", None, None),
        P("dp", "ctx", None),
        P("dp", "ctx", None),
        P(),
        P("dp", "ctx"),
        P("dp", None),
        P(),
        P("dp", "ctx", None, None),
        P("dp", "ctx", None, None),
        P("dp", "ctx", None),
        P(None, "ctx", None),
        P(None, "ctx", None),
    )
    return jax.shard_map(
        shards,
        mesh=mesh,
        in_specs=placed,
        out_specs=(P("dp", "ctx", None, None), P("dp", "ctx", None, None), P()),
        check_vma=False,
    )
```

profile of v0, /device:TPU:1, one launch (start us, length us, event | category | flops | bytes accessed | tf_op | source)
XLA Modules:
  0.0 411.5 jit_solution(6213377689688391206)
XLA Ops:
  7.2 1.4 collective-permute-start.5
  8.7 1.3 collective-permute-start.4
  10.0 7.0 %collective-permute-start.7 = (bf16[1,128,512]{2,1,0:T(8,128)(2,1)}, bf16[1,128,512]{2,1,0:T(8,128)(2,1)S(1)}, u32[]{:S(2)}, u32[]{:S(2)}) collective-permute-start(bf16[1,128,512]{2,1,0:T(8,128)(2,1)} %param.25), channel_id=1, source_target_pairs={{0,2},{1,3},{2,4},{3,5},{4,6},{5,7},{6,8},{7,9},{8,10},{9,11},{10,... | collective-permute-start | bytes 393224 | tf_op jit(solution)/shard_map/ppermute | solution.py:15
  16.9 1.5 copy.62
  18.6 1.5 broadcast_select_fusion.5
  21.0 1.3 constant_dynamic-slice_fusion.7
  30.9 1.5 multiply_bitcast_fusion
  32.4 3.1 fusion.27
  35.4 158.9 %custom-call.4 = f32[1,2,16,1,64,64]{4,5,3,2,1,0:T(8,128)} custom-call(f32[1,2,16,1,64,64]{5,4,3,2,1,0:T(8,128)} %fusion.27), custom_call_target="InvertDiagBlocksLowerTriangular" | custom-call | tf_op jit(solution)/shard_map/vmap(vmap(jit(_solve_triangular)))/vmap()/triangular_solve | solution.py:41
  195.9 2.0 fusion.10
  198.0 3.6 convolution_bitcast_fusion
  201.6 4.0 subtract_bitcast_fusion
  205.6 2.0 fusion.20
  207.7 1.9 collective-permute-start.2
  209.6 2.0 fusion.22
  211.6 5.0 %collective-permute-start = (f32[1,16,128,128]{3,2,1,0:T(8,128)}, f32[1,16,128,128]{3,2,1,0:T(8,128)}, u32[]{:S(2)}, u32[]{:S(2)}) collective-permute-start(f32[1,16,128,128]{3,2,1,0:T(8,128)} %fusion.22), channel_id=1, source_target_pairs={{0,1},{1,2},{2,3},{3,4},{4,5},{5,6},{6,7},{7,8},{8,9},{9,10},{10,1... | collective-permute-start | bytes 3145736 | tf_op jit(solution)/shard_map/ppermute | solution.py:15
  217.6 2.1 convolution_multiply_fusion.2
  221.0 1.5 fusion.29
  222.5 5.7 %collective-permute-done.2 = f32[1,16,128,128]{3,2,1,0:T(8,128)} collective-permute-done((f32[1,16,128,128]{3,2,1,0:T(8,128)}, f32[1,16,128,128]{3,2,1,0:T(8,128)}, u32[]{:S(2)}, u32[]{:S(2)}) %collective-permute-start.2) | collective-permute-done | bytes 1048608 | tf_op jit(solution)/shard_map/ppermute | solution.py:15
  228.2 3.5 fusion.19
  231.7 1.4 collective-permute-start.3
  233.1 2.4 fusion.21
  235.5 5.8 %collective-permute-start.1 = (f32[1,16,128,128]{3,2,1,0:T(8,128)S(1)}, f32[1,16,128,128]{3,2,1,0:T(8,128)}, u32[]{:S(2)}, u32[]{:S(2)}) collective-permute-start(f32[1,16,128,128]{3,2,1,0:T(8,128)S(1)} %fusion.21), channel_id=1, source_target_pairs={{0,1},{1,2},{2,3},{3,4},{4,5},{5,6},{6,7},{7,8},{8,9},{9,10},{10,1... | collective-permute-start | bytes 3145736 | tf_op jit(solution)/shard_map/ppermute | solution.py:15
  242.0 5.8 %collective-permute-start.6 = (bf16[1,128,512]{2,1,0:T(8,128)(2,1)S(1)}, bf16[1,128,512]{2,1,0:T(8,128)(2,1)S(1)}, u32[]{:S(2)}, u32[]{:S(2)}) collective-permute-start(bf16[1,128,512]{2,1,0:T(8,128)(2,1)S(1)} %copy-done.12), channel_id=1, source_target_pairs={{0,1},{1,2},{2,3},{3,4},{4,5},{5,6},{6,7},{7,8},{8,9},{9,10},{10,1... | collective-permute-start | bytes 393224 | tf_op jit(solution)/shard_map/ppermute | solution.py:15
  248.8 11.5 %collective-permute-done.6 = bf16[1,128,512]{2,1,0:T(8,128)(2,1)S(1)} collective-permute-done((bf16[1,128,512]{2,1,0:T(8,128)(2,1)S(1)}, bf16[1,128,512]{2,1,0:T(8,128)(2,1)S(1)}, u32[]{:S(2)}, u32[]{:S(2)}) %collective-permute-start.6) | collective-permute-done | bytes 131104 | tf_op jit(solution)/shard_map/ppermute | solution.py:15
  260.5 1.3 select_bitcast_fusion
  261.8 3.3 multiply_reduce_fusion.1
  266.1 1.2 multiply_reduce_fusion
  267.3 124.6 %psum.7 = f32[128]{0:T(128)S(1)} all-reduce(f32[128]{0:T(128)S(1)} %get-tuple-element.17), channel_id=1, replica_groups=mesh['dp'=16,'ctx'=32] {'dp','ctx'}, use_global_device_ids=true, to_apply=%region_8.9 | all-reduce | flops 128 | bytes 1024 | tf_op jit(solution)/shard_map/psum | solution.py:145
  392.4 4.2 %convert_bitcast_fusion = bf16[1,128,16,512]{3,1,2,0:T(8,128)(2,1)S(1)} fusion(bf16[16,128,512]{2,0,1:T(8,128)(2,1)} %all-gather.3.cloned.1.call-done, bf16[128,16,128]{2,1,0:T(8,128)(2,1)S(1)} %bitcast.248), kind=kOutput, calls=%fused_computation.10 | convolution fusion | flops 269484032 | bytes 4718592 | tf_op jit(solution)/shard_map/sthn,hnl->sthl/dot_general | solution.py:161
  398.5 2.4 fusion.34
  400.9 2.4 fusion.35
  (135 shorter events, 18.4 us)
Async XLA Ops:
  7.2 21.9 %copy-start.7 = (bf16[1,128,16,128]{3,2,1,0:T(8,128)(2,1)S(1)}, bf16[1,128,16,128]{3,2,1,0:T(8,128)(2,1)}, u32[]{:S(2)}) copy-start(bf16[1,128,16,128]{3,2,1,0:T(8,128)(2,1)} %param.15) | copy-start | bytes 1572868
  7.2 385.2 %all-gather.3.cloned.1.call-start = ((), (), s32[]{:S(2)}) async-start(), calls=%async_computation | async-start | bytes 2162688 | tf_op jit(solution)/shard_map/all_gather | solution.py:158
  7.2 241.6 %collective-permute-start.5 = (bf16[1,128,512]{2,1,0:T(8,128)(2,1)}, bf16[1,128,512]{2,1,0:T(8,128)(2,1)S(1)}, u32[]{:S(2)}, u32[]{:S(2)}) collective-permute-start(bf16[1,128,512]{2,1,0:T(8,128)(2,1)} %param.25), channel_id=1, source_target_pairs={{1,0},{2,1},{3,2},{4,3},{5,4},{6,5},{7,6},{8,7},{9,8},{10,9},{11,1... | collective-permute-start | bytes 393224 | tf_op jit(solution)/shard_map/ppermute | solution.py:15
  8.7 233.4 %collective-permute-start.4 = (bf16[1,128,512]{2,1,0:T(8,128)(2,1)}, bf16[1,128,512]{2,1,0:T(8,128)(2,1)}, u32[]{:S(2)}, u32[]{:S(2)}) collective-permute-start(bf16[1,128,512]{2,1,0:T(8,128)(2,1)} %param.25), channel_id=1, source_target_pairs={{2,0},{3,1},{4,2},{5,3},{6,4},{7,5},{8,6},{9,7},{10,8},{11,9},{12,... | collective-permute-start | bytes 393224 | tf_op jit(solution)/shard_map/ppermute | solution.py:15
  10.0 250.4 %collective-permute-start.7 = (bf16[1,128,512]{2,1,0:T(8,128)(2,1)}, bf16[1,128,512]{2,1,0:T(8,128)(2,1)S(1)}, u32[]{:S(2)}, u32[]{:S(2)}) collective-permute-start(bf16[1,128,512]{2,1,0:T(8,128)(2,1)} %param.25), channel_id=1, source_target_pairs={{0,2},{1,3},{2,4},{3,5},{4,6},{5,7},{6,8},{7,9},{8,10},{9,11},{10,... | collective-permute-start | bytes 393224 | tf_op jit(solution)/shard_map/ppermute | solution.py:15
  18.4 380.0 %all-gather.5.cloned.1.call-start = ((), (), s32[]{:S(2)}) async-start(), calls=%async_computation.1 | async-start | bytes 2162688 | tf_op jit(solution)/shard_map/all_gather | solution.py:159
  20.1 7.1 %copy-start.15 = (s32[1,64]{1,0:T(1,128)}, s32[1,64]{1,0:T(1,128)S(1)}, u32[]{:S(2)}) copy-start(s32[1,64]{1,0:T(1,128)S(1)} %get-tuple-element.29) | copy-start | bytes 772
  20.1 7.1 %copy-start.17 = (s32[1,64]{1,0:T(1,128)}, s32[1,64]{1,0:T(1,128)S(1)}, u32[]{:S(2)}) copy-start(s32[1,64]{1,0:T(1,128)S(1)} %get-tuple-element.30) | copy-start | bytes 772
  23.5 3.7 copy-start.30
  24.2 5.3 %copy-start.20 = (f32[2,64]{1,0:T(2,128)}, f32[2,64]{1,0:T(2,128)S(1)}, u32[]{:S(2)}) copy-start(f32[2,64]{1,0:T(2,128)S(1)} %get-tuple-element.38) | copy-start | bytes 1540
  197.9 3.7 copy-start
  201.5 8.0 %copy-start.2 = (f32[1,2,16,128,128]{4,3,2,1,0:T(8,128)}, f32[1,2,16,128,128]{4,3,2,1,0:T(8,128)S(1)}, u32[]{:S(2)}) copy-start(f32[1,2,16,128,128]{4,3,2,1,0:T(8,128)S(1)} %convolution_bitcast_fusion) | copy-start | bytes 6291460
  205.6 5.9 %copy-start.4 = (f32[1,2,16,128,128]{4,3,2,1,0:T(8,128)}, f32[1,2,16,128,128]{4,3,2,1,0:T(8,128)S(1)}, u32[]{:S(2)}) copy-start(f32[1,2,16,128,128]{4,3,2,1,0:T(8,128)S(1)} %subtract_bitcast_fusion) | copy-start | bytes 6291460
  207.6 9.0 %copy-start.8 = (bf16[1,128,16,128]{3,2,1,0:T(8,128)(2,1)S(1)}, bf16[1,128,16,128]{3,2,1,0:T(8,128)(2,1)}, u32[]{:S(2)}) copy-start(bf16[1,128,16,128]{3,2,1,0:T(8,128)(2,1)} %param.14) | copy-start | bytes 1572868
  207.6 9.8 %copy-start.22 = (s32[1,64]{1,0:T(1,128)S(1)}, s32[1,64]{1,0:T(1,128)}, u32[]{:S(2)}) copy-start(s32[1,64]{1,0:T(1,128)} %get-tuple-element.25) | copy-start | bytes 772
  207.6 9.8 %copy-start.23 = (s32[1,64]{1,0:T(1,128)S(1)}, s32[1,64]{1,0:T(1,128)}, u32[]{:S(2)}) copy-start(s32[1,64]{1,0:T(1,128)} %get-tuple-element.26) | copy-start | bytes 772
  207.6 9.8 %copy-start.24 = (s32[1,64]{1,0:T(1,128)S(1)}, s32[1,64]{1,0:T(1,128)}, u32[]{:S(2)}) copy-start(s32[1,64]{1,0:T(1,128)} %get-tuple-element.27) | copy-start | bytes 772
  207.6 9.8 %copy-start.25 = (s32[1,64]{1,0:T(1,128)S(1)}, s32[1,64]{1,0:T(1,128)}, u32[]{:S(2)}) copy-start(s32[1,64]{1,0:T(1,128)} %get-tuple-element.28) | copy-start | bytes 772
  207.6 9.8 %copy-start.26 = (s32[1,64]{1,0:T(1,128)S(1)}, s32[1,64]{1,0:T(1,128)}, u32[]{:S(2)}) copy-start(s32[1,64]{1,0:T(1,128)} %get-tuple-element.31) | copy-start | bytes 772
  207.7 9.8 %copy-start.27 = (s32[1,64]{1,0:T(1,128)S(1)}, s32[1,64]{1,0:T(1,128)}, u32[]{:S(2)}) copy-start(s32[1,64]{1,0:T(1,128)} %get-tuple-element.32) | copy-start | bytes 772
  207.7 20.5 %collective-permute-start.2 = (f32[1,16,128,128]{3,2,1,0:T(8,128)}, f32[1,16,128,128]{3,2,1,0:T(8,128)}, u32[]{:S(2)}, u32[]{:S(2)}) collective-permute-start(f32[1,16,128,128]{3,2,1,0:T(8,128)} %fusion.20), channel_id=1, source_target_pairs={{1,0},{2,1},{3,2},{4,3},{5,4},{6,5},{7,6},{8,7},{9,8},{10,9},{11,1... | collective-permute-start | bytes 3145736 | tf_op jit(solution)/shard_map/ppermute | solution.py:15
  211.6 21.5 %collective-permute-start = (f32[1,16,128,128]{3,2,1,0:T(8,128)}, f32[1,16,128,128]{3,2,1,0:T(8,128)}, u32[]{:S(2)}, u32[]{:S(2)}) collective-permute-start(f32[1,16,128,128]{3,2,1,0:T(8,128)} %fusion.22), channel_id=1, source_target_pairs={{0,1},{1,2},{2,3},{3,4},{4,5},{5,6},{6,7},{7,8},{8,9},{9,10},{10,1... | collective-permute-start | bytes 3145736 | tf_op jit(solution)/shard_map/ppermute | solution.py:15
  216.6 3.2 copy-start.28
  221.0 7.2 %copy-start.3 = (f32[1,2,16,128,128]{4,3,2,1,0:T(8,128)S(1)}, f32[1,2,16,128,128]{4,3,2,1,0:T(8,128)}, u32[]{:S(2)}) copy-start(f32[1,2,16,128,128]{4,3,2,1,0:T(8,128)} %copy-done.2) | copy-start | bytes 6291460
  221.0 7.2 %copy-start.5 = (f32[1,2,16,128,128]{4,3,2,1,0:T(8,128)S(1)}, f32[1,2,16,128,128]{4,3,2,1,0:T(8,128)}, u32[]{:S(2)}) copy-start(f32[1,2,16,128,128]{4,3,2,1,0:T(8,128)} %copy-done.4) | copy-start | bytes 6291460
  231.7 9.7 %copy-start.16 = (s32[1,64]{1,0:T(1,128)S(1)}, s32[1,64]{1,0:T(1,128)}, u32[]{:S(2)}) copy-start(s32[1,64]{1,0:T(1,128)} %copy-done.15) | copy-start | bytes 772
  231.7 9.7 %copy-start.29 = (s32[64]{0:T(128)S(1)}, s32[64]{0:T(128)}, u32[]{:S(2)}) copy-start(s32[64]{0:T(128)} %copy-done.28) | copy-start | bytes 772
  231.7 10.4 %copy-start.12 = (bf16[1,128,512]{2,1,0:T(8,128)(2,1)S(1)}, bf16[1,128,512]{2,1,0:T(8,128)(2,1)}, u32[]{:S(2)}) copy-start(bf16[1,128,512]{2,1,0:T(8,128)(2,1)} %param.25) | copy-start | bytes 393220
  231.7 28.8 %collective-permute-start.3 = (f32[1,16,128,128]{3,2,1,0:T(8,128)}, f32[1,16,128,128]{3,2,1,0:T(8,128)}, u32[]{:S(2)}, u32[]{:S(2)}) collective-permute-start(f32[1,16,128,128]{3,2,1,0:T(8,128)} %fusion.19), channel_id=1, source_target_pairs={{1,0},{2,1},{3,2},{4,3},{5,4},{6,5},{7,6},{8,7},{9,8},{10,9},{11,1... | collective-permute-start | bytes 3145736 | tf_op jit(solution)/shard_map/ppermute | solution.py:15
  235.5 26.3 %collective-permute-start.1 = (f32[1,16,128,128]{3,2,1,0:T(8,128)S(1)}, f32[1,16,128,128]{3,2,1,0:T(8,128)}, u32[]{:S(2)}, u32[]{:S(2)}) collective-permute-start(f32[1,16,128,128]{3,2,1,0:T(8,128)S(1)} %fusion.21), channel_id=1, source_target_pairs={{0,1},{1,2},{2,3},{3,4},{4,5},{5,6},{6,7},{7,8},{8,9},{9,10},{10,1... | collective-permute-start | bytes 3145736 | tf_op jit(solution)/shard_map/ppermute | solution.py:15
  242.0 18.3 %collective-permute-start.6 = (bf16[1,128,512]{2,1,0:T(8,128)(2,1)S(1)}, bf16[1,128,512]{2,1,0:T(8,128)(2,1)S(1)}, u32[]{:S(2)}, u32[]{:S(2)}) collective-permute-start(bf16[1,128,512]{2,1,0:T(8,128)(2,1)S(1)} %copy-done.12), channel_id=1, source_target_pairs={{0,1},{1,2},{2,3},{3,4},{4,5},{5,6},{6,7},{7,8},{8,9},{9,10},{10,1... | collective-permute-start | bytes 393224 | tf_op jit(solution)/shard_map/ppermute | solution.py:15
  265.2 127.2 %copy-start.10 = (bf16[1,128,16,128]{3,2,1,0:T(8,128)(2,1)S(1)}, bf16[1,128,16,128]{3,2,1,0:T(8,128)(2,1)}, u32[]{:S(2)}) copy-start(bf16[1,128,16,128]{3,2,1,0:T(8,128)(2,1)} %param.24) | copy-start | bytes 1572868
  (10 other events, 15.3 us)
Sparse Core Ops, SparseCore 0:
  18.6 86.8 all-gather.2
  216.7 88.3 all-gather.4
where the time goes:
time: 417 us; the launch traced here: 411 us
  other arithmetic  174 us (42%)
  blocking collectives  125 us (30%)
  matrix products  41.3 us (10%)
  starting transfers between devices  29.7 us (7%)
  waiting for transfers between devices  17.3 us (4%)
  between operations  16.2 us (4%)
  local copies, waits for them, and re-layouts  8.72 us (2%)
    another operation x4, other arithmetic, block_maps(): jax.scipy.linalg.solve_triangular(identity_mat[None] + triangle, jnp.tran...  160 us
    psum x1, blocking collectives, shards(): total_grad = lax.psum(partial_grad, ('dp', 'ctx'))  125 us
    ppermute x8, starting transfers between devices, from_behind(): lax.ppermute(value, axis, [(source, source + steps) for source in range(l...  29.6 us
    ppermute x8, waiting for transfers between devices, from_behind(): lax.ppermute(value, axis, [(source, source + steps) for source in range(l...  17.3 us
    dot_general x4, matrix products, advance(): jnp.einsum('shcd,shdv->shcv', transfer_map, state, precision=exact_mode)  9.83 us
  transfers between devices with their start and end apart: 10, of which 2 were waited for; matrix products, arithmetic and copies ran while one was open for 53% of the time, Pallas kernels for 0%

commit v1 on v0

--- a/solution.py
+++ b/solution.py
@@ -142,7 +142,7 @@
     normed = kda_raw * lax.rsqrt(meansq + 1e-06)
     kda_output = (normed * delta_norm_gain).astype(jnp.bfloat16)
     partial_grad = jnp.sum(normed * delta_output_cotangent.astype(jnp.float32), axis=(0, 1, 2))
-    total_grad = lax.psum(partial_grad, ("dp", "ctx"))
+    total_grad = lax.psum(lax.psum(partial_grad, "ctx"), "dp")
     gain_grad = total_grad / math.sqrt(seqs * lax.axis_size("dp") * rows * ranks * heads)
     latent_width = compressed_latents.shape[2]
     neighbours = {0: compressed_latents}

time: 417 us -> 406 us (0.974)
  blocking collectives: 125 us -> 117 us
    psum x1 -> x2, blocking collectives: 125 us -> 117 us  [shards(): total_grad = lax.psum(lax.psum(partial_grad, 'ctx'), 'dp')]
  transfers between devices with their start and end apart: 10 -> 10, of which waited for: 2 -> 2; matrix products, arithmetic and copies ran while one was open for 53% -> 54% of each run, Pallas kernels for 0% -> 0%
where the time goes in v1:
time: 406 us; the launch traced here: 403 us
  other arithmetic  174 us (43%)
  blocking collectives  117 us (29%)
  matrix products  41.3 us (10%)
  starting transfers between devices  29.5 us (7%)
  waiting for transfers between devices  17.1 us (4%)
  between operations  16.1 us (4%)
  local copies, waits for them, and re-layouts  8.74 us (2%)
    another operation x4, other arithmetic, block_maps(): jax.scipy.linalg.solve_triangular(identity_mat[None] + triangle, jnp.tran...  159 us
    psum x2, blocking collectives, shards(): total_grad = lax.psum(lax.psum(partial_grad, 'ctx'), 'dp')  117 us
    ppermute x8, starting transfers between devices, from_behind(): lax.ppermute(value, axis, [(source, source + steps) for source in range(l...  29.5 us
    ppermute x8, waiting for transfers between devices, from_behind(): lax.ppermute(value, axis, [(source, source + steps) for source in range(l...  17.1 us
    dot_general x4, matrix products, advance(): jnp.einsum('shcd,shdv->shcv', transfer_map, state, precision=exact_mode)  9.82 us
  transfers between devices with their start and end apart: 10, of which 2 were waited for; matrix products, arithmetic and copies ran while one was open for 54% of the time, Pallas kernels for 0%

profile of v1, /device:TPU:1, one launch (start us, length us, event | category | flops | bytes accessed | tf_op | source)
XLA Modules:
  0.0 403.4 jit_solution(15819941428707871163)
XLA Ops:
  7.2 1.4 collective-permute-start.5
  8.7 1.3 collective-permute-start.4
  10.0 7.0 %collective-permute-start.7 = (bf16[1,128,512]{2,1,0:T(8,128)(2,1)}, bf16[1,128,512]{2,1,0:T(8,128)(2,1)S(1)}, u32[]{:S(2)}, u32[]{:S(2)}) collective-permute-start(bf16[1,128,512]{2,1,0:T(8,128)(2,1)} %param.25), channel_id=1, source_target_pairs={{0,2},{1,3},{2,4},{3,5},{4,6},{5,7},{6,8},{7,9},{8,10},{9,11},{10,... | collective-permute-start | bytes 393224 | tf_op jit(solution)/shard_map/ppermute | solution.py:15
  16.9 1.5 copy.62
  18.6 1.5 broadcast_select_fusion.5
  21.0 1.3 constant_dynamic-slice_fusion.7
  31.0 1.5 multiply_bitcast_fusion
  32.6 3.0 fusion.27
  35.6 158.7 %custom-call.4 = f32[1,2,16,1,64,64]{4,5,3,2,1,0:T(8,128)} custom-call(f32[1,2,16,1,64,64]{5,4,3,2,1,0:T(8,128)} %fusion.27), custom_call_target="InvertDiagBlocksLowerTriangular" | custom-call | tf_op jit(solution)/shard_map/vmap(vmap(jit(_solve_triangular)))/vmap()/triangular_solve | solution.py:41
  195.8 2.0 fusion.10
  197.9 3.6 convolution_bitcast_fusion
  201.5 4.0 subtract_bitcast_fusion
  205.6 2.0 fusion.20
  207.6 1.6 collective-permute-start.2
  209.3 2.0 fusion.22
  211.2 5.0 %collective-permute-start = (f32[1,16,128,128]{3,2,1,0:T(8,128)}, f32[1,16,128,128]{3,2,1,0:T(8,128)}, u32[]{:S(2)}, u32[]{:S(2)}) collective-permute-start(f32[1,16,128,128]{3,2,1,0:T(8,128)} %fusion.22), channel_id=1, source_target_pairs={{0,1},{1,2},{2,3},{3,4},{4,5},{5,6},{6,7},{7,8},{8,9},{9,10},{10,1... | collective-permute-start | bytes 3145736 | tf_op jit(solution)/shard_map/ppermute | solution.py:15
  217.3 2.1 convolution_multiply_fusion.2
  220.7 1.5 fusion.29
  222.1 6.0 %collective-permute-done.2 = f32[1,16,128,128]{3,2,1,0:T(8,128)} collective-permute-done((f32[1,16,128,128]{3,2,1,0:T(8,128)}, f32[1,16,128,128]{3,2,1,0:T(8,128)}, u32[]{:S(2)}, u32[]{:S(2)}) %collective-permute-start.2) | collective-permute-done | bytes 1048608 | tf_op jit(solution)/shard_map/ppermute | solution.py:15
  228.1 3.4 fusion.19
  231.6 1.4 collective-permute-start.3
  233.0 2.4 fusion.21
  235.4 5.9 %collective-permute-start.1 = (f32[1,16,128,128]{3,2,1,0:T(8,128)S(1)}, f32[1,16,128,128]{3,2,1,0:T(8,128)}, u32[]{:S(2)}, u32[]{:S(2)}) collective-permute-start(f32[1,16,128,128]{3,2,1,0:T(8,128)S(1)} %fusion.21), channel_id=1, source_target_pairs={{0,1},{1,2},{2,3},{3,4},{4,5},{5,6},{6,7},{7,8},{8,9},{9,10},{10,1... | collective-permute-start | bytes 3145736 | tf_op jit(solution)/shard_map/ppermute | solution.py:15
  242.0 5.9 %collective-permute-start.6 = (bf16[1,128,512]{2,1,0:T(8,128)(2,1)S(1)}, bf16[1,128,512]{2,1,0:T(8,128)(2,1)S(1)}, u32[]{:S(2)}, u32[]{:S(2)}) collective-permute-start(bf16[1,128,512]{2,1,0:T(8,128)(2,1)S(1)} %copy-done.12), channel_id=1, source_target_pairs={{0,1},{1,2},{2,3},{3,4},{4,5},{5,6},{6,7},{7,8},{8,9},{9,10},{10,1... | collective-permute-start | bytes 393224 | tf_op jit(solution)/shard_map/ppermute | solution.py:15
  248.8 11.1 %collective-permute-done.6 = bf16[1,128,512]{2,1,0:T(8,128)(2,1)S(1)} collective-permute-done((bf16[1,128,512]{2,1,0:T(8,128)(2,1)S(1)}, bf16[1,128,512]{2,1,0:T(8,128)(2,1)S(1)}, u32[]{:S(2)}, u32[]{:S(2)}) %collective-permute-start.6) | collective-permute-done | bytes 131104 | tf_op jit(solution)/shard_map/ppermute | solution.py:15
  260.0 1.3 select_bitcast_fusion
  261.4 3.3 multiply_reduce_fusion.1
  266.9 76.1 %psum.14 = f32[128]{0:T(128)S(1)} all-reduce(f32[128]{0:T(128)S(1)} %get-tuple-element.17), channel_id=1, replica_groups=mesh['dp'=16,'ctx'=32] {'ctx'}, use_global_device_ids=true, to_apply=%region_8.9 | all-reduce | flops 128 | bytes 1024 | tf_op jit(solution)/shard_map/psum | solution.py:145
  343.0 41.0 %psum.15 = f32[128]{0:T(128)S(1)} all-reduce(f32[128]{0:T(128)S(1)} %psum.14), channel_id=1, replica_groups=mesh['dp'=16,'ctx'=32] {'dp'}, use_global_device_ids=true, to_apply=%region_9.10 | all-reduce | flops 128 | bytes 1024 | tf_op jit(solution)/shard_map/psum | solution.py:145
  384.5 4.2 %convert_bitcast_fusion = bf16[1,128,16,512]{3,1,2,0:T(8,128)(2,1)S(1)} fusion(bf16[16,128,512]{2,0,1:T(8,128)(2,1)} %all-gather.3.cloned.1.call-done, bf16[128,16,128]{2,1,0:T(8,128)(2,1)S(1)} %bitcast.248), kind=kOutput, calls=%fused_computation.10 | convolution fusion | flops 269484032 | bytes 4718592 | tf_op jit(solution)/shard_map/sthn,hnl->sthl/dot_general | solution.py:161
  390.6 2.4 fusion.34
  393.0 2.4 fusion.35
  (136 shorter events, 19.6 us)
Async XLA Ops:
  7.2 22.1 %copy-start.7 = (bf16[1,128,16,128]{3,2,1,0:T(8,128)(2,1)S(1)}, bf16[1,128,16,128]{3,2,1,0:T(8,128)(2,1)}, u32[]{:S(2)}) copy-start(bf16[1,128,16,128]{3,2,1,0:T(8,128)(2,1)} %param.15) | copy-start | bytes 1572868
  7.2 377.3 %all-gather.3.cloned.1.call-start = ((), (), s32[]{:S(2)}) async-start(), calls=%async_computation | async-start | bytes 2162688 | tf_op jit(solution)/shard_map/all_gather | solution.py:158
  7.2 241.5 %collective-permute-start.5 = (bf16[1,128,512]{2,1,0:T(8,128)(2,1)}, bf16[1,128,512]{2,1,0:T(8,128)(2,1)S(1)}, u32[]{:S(2)}, u32[]{:S(2)}) collective-permute-start(bf16[1,128,512]{2,1,0:T(8,128)(2,1)} %param.25), channel_id=1, source_target_pairs={{1,0},{2,1},{3,2},{4,3},{5,4},{6,5},{7,6},{8,7},{9,8},{10,9},{11,1... | collective-permute-start | bytes 393224 | tf_op jit(solution)/shard_map/ppermute | solution.py:15
  8.7 233.3 %collective-permute-start.4 = (bf16[1,128,512]{2,1,0:T(8,128)(2,1)}, bf16[1,128,512]{2,1,0:T(8,128)(2,1)}, u32[]{:S(2)}, u32[]{:S(2)}) collective-permute-start(bf16[1,128,512]{2,1,0:T(8,128)(2,1)} %param.25), channel_id=1, source_target_pairs={{2,0},{3,1},{4,2},{5,3},{6,4},{7,5},{8,6},{9,7},{10,8},{11,9},{12,... | collective-permute-start | bytes 393224 | tf_op jit(solution)/shard_map/ppermute | solution.py:15
  10.0 250.0 %collective-permute-start.7 = (bf16[1,128,512]{2,1,0:T(8,128)(2,1)}, bf16[1,128,512]{2,1,0:T(8,128)(2,1)S(1)}, u32[]{:S(2)}, u32[]{:S(2)}) collective-permute-start(bf16[1,128,512]{2,1,0:T(8,128)(2,1)} %param.25), channel_id=1, source_target_pairs={{0,2},{1,3},{2,4},{3,5},{4,6},{5,7},{6,8},{7,9},{8,10},{9,11},{10,... | collective-permute-start | bytes 393224 | tf_op jit(solution)/shard_map/ppermute | solution.py:15
  18.4 372.1 %all-gather.5.cloned.1.call-start = ((), (), s32[]{:S(2)}) async-start(), calls=%async_computation.1 | async-start | bytes 2162688 | tf_op jit(solution)/shard_map/all_gather | solution.py:159
  20.1 7.3 %copy-start.15 = (s32[1,64]{1,0:T(1,128)}, s32[1,64]{1,0:T(1,128)S(1)}, u32[]{:S(2)}) copy-start(s32[1,64]{1,0:T(1,128)S(1)} %get-tuple-element.29) | copy-start | bytes 772
  20.1 7.3 %copy-start.17 = (s32[1,64]{1,0:T(1,128)}, s32[1,64]{1,0:T(1,128)S(1)}, u32[]{:S(2)}) copy-start(s32[1,64]{1,0:T(1,128)S(1)} %get-tuple-element.30) | copy-start | bytes 772
  23.7 3.7 copy-start.30
  24.4 5.3 %copy-start.20 = (f32[2,64]{1,0:T(2,128)}, f32[2,64]{1,0:T(2,128)S(1)}, u32[]{:S(2)}) copy-start(f32[2,64]{1,0:T(2,128)S(1)} %get-tuple-element.38) | copy-start | bytes 1540
  197.8 3.7 copy-start
  201.5 7.8 %copy-start.2 = (f32[1,2,16,128,128]{4,3,2,1,0:T(8,128)}, f32[1,2,16,128,128]{4,3,2,1,0:T(8,128)S(1)}, u32[]{:S(2)}) copy-start(f32[1,2,16,128,128]{4,3,2,1,0:T(8,128)S(1)} %convolution_bitcast_fusion) | copy-start | bytes 6291460
  205.6 5.7 %copy-start.4 = (f32[1,2,16,128,128]{4,3,2,1,0:T(8,128)}, f32[1,2,16,128,128]{4,3,2,1,0:T(8,128)S(1)}, u32[]{:S(2)}) copy-start(f32[1,2,16,128,128]{4,3,2,1,0:T(8,128)S(1)} %subtract_bitcast_fusion) | copy-start | bytes 6291460
  207.6 8.8 %copy-start.8 = (bf16[1,128,16,128]{3,2,1,0:T(8,128)(2,1)S(1)}, bf16[1,128,16,128]{3,2,1,0:T(8,128)(2,1)}, u32[]{:S(2)}) copy-start(bf16[1,128,16,128]{3,2,1,0:T(8,128)(2,1)} %param.14) | copy-start | bytes 1572868
  207.6 9.5 %copy-start.22 = (s32[1,64]{1,0:T(1,128)S(1)}, s32[1,64]{1,0:T(1,128)}, u32[]{:S(2)}) copy-start(s32[1,64]{1,0:T(1,128)} %get-tuple-element.25) | copy-start | bytes 772
  207.6 9.5 %copy-start.23 = (s32[1,64]{1,0:T(1,128)S(1)}, s32[1,64]{1,0:T(1,128)}, u32[]{:S(2)}) copy-start(s32[1,64]{1,0:T(1,128)} %get-tuple-element.26) | copy-start | bytes 772
  207.6 9.5 %copy-start.24 = (s32[1,64]{1,0:T(1,128)S(1)}, s32[1,64]{1,0:T(1,128)}, u32[]{:S(2)}) copy-start(s32[1,64]{1,0:T(1,128)} %get-tuple-element.27) | copy-start | bytes 772
  207.6 9.5 %copy-start.25 = (s32[1,64]{1,0:T(1,128)S(1)}, s32[1,64]{1,0:T(1,128)}, u32[]{:S(2)}) copy-start(s32[1,64]{1,0:T(1,128)} %get-tuple-element.28) | copy-start | bytes 772
  207.6 9.5 %copy-start.26 = (s32[1,64]{1,0:T(1,128)S(1)}, s32[1,64]{1,0:T(1,128)}, u32[]{:S(2)}) copy-start(s32[1,64]{1,0:T(1,128)} %get-tuple-element.31) | copy-start | bytes 772
  207.6 9.5 %copy-start.27 = (s32[1,64]{1,0:T(1,128)S(1)}, s32[1,64]{1,0:T(1,128)}, u32[]{:S(2)}) copy-start(s32[1,64]{1,0:T(1,128)} %get-tuple-element.32) | copy-start | bytes 772
  207.6 20.5 %collective-permute-start.2 = (f32[1,16,128,128]{3,2,1,0:T(8,128)}, f32[1,16,128,128]{3,2,1,0:T(8,128)}, u32[]{:S(2)}, u32[]{:S(2)}) collective-permute-start(f32[1,16,128,128]{3,2,1,0:T(8,128)} %fusion.20), channel_id=1, source_target_pairs={{1,0},{2,1},{3,2},{4,3},{5,4},{6,5},{7,6},{8,7},{9,8},{10,9},{11,1... | collective-permute-start | bytes 3145736 | tf_op jit(solution)/shard_map/ppermute | solution.py:15
  211.2 21.7 %collective-permute-start = (f32[1,16,128,128]{3,2,1,0:T(8,128)}, f32[1,16,128,128]{3,2,1,0:T(8,128)}, u32[]{:S(2)}, u32[]{:S(2)}) collective-permute-start(f32[1,16,128,128]{3,2,1,0:T(8,128)} %fusion.22), channel_id=1, source_target_pairs={{0,1},{1,2},{2,3},{3,4},{4,5},{5,6},{6,7},{7,8},{8,9},{9,10},{10,1... | collective-permute-start | bytes 3145736 | tf_op jit(solution)/shard_map/ppermute | solution.py:15
  216.3 3.2 copy-start.28
  220.7 7.4 %copy-start.3 = (f32[1,2,16,128,128]{4,3,2,1,0:T(8,128)S(1)}, f32[1,2,16,128,128]{4,3,2,1,0:T(8,128)}, u32[]{:S(2)}) copy-start(f32[1,2,16,128,128]{4,3,2,1,0:T(8,128)} %copy-done.2) | copy-start | bytes 6291460
  220.7 7.4 %copy-start.5 = (f32[1,2,16,128,128]{4,3,2,1,0:T(8,128)S(1)}, f32[1,2,16,128,128]{4,3,2,1,0:T(8,128)}, u32[]{:S(2)}) copy-start(f32[1,2,16,128,128]{4,3,2,1,0:T(8,128)} %copy-done.4) | copy-start | bytes 6291460
  231.6 9.7 %copy-start.16 = (s32[1,64]{1,0:T(1,128)S(1)}, s32[1,64]{1,0:T(1,128)}, u32[]{:S(2)}) copy-start(s32[1,64]{1,0:T(1,128)} %copy-done.15) | copy-start | bytes 772
  231.6 9.7 %copy-start.29 = (s32[64]{0:T(128)S(1)}, s32[64]{0:T(128)}, u32[]{:S(2)}) copy-start(s32[64]{0:T(128)} %copy-done.28) | copy-start | bytes 772
  231.6 10.4 %copy-start.12 = (bf16[1,128,512]{2,1,0:T(8,128)(2,1)S(1)}, bf16[1,128,512]{2,1,0:T(8,128)(2,1)}, u32[]{:S(2)}) copy-start(bf16[1,128,512]{2,1,0:T(8,128)(2,1)} %param.25) | copy-start | bytes 393220
  231.6 28.5 %collective-permute-start.3 = (f32[1,16,128,128]{3,2,1,0:T(8,128)}, f32[1,16,128,128]{3,2,1,0:T(8,128)}, u32[]{:S(2)}, u32[]{:S(2)}) collective-permute-start(f32[1,16,128,128]{3,2,1,0:T(8,128)} %fusion.19), channel_id=1, source_target_pairs={{1,0},{2,1},{3,2},{4,3},{5,4},{6,5},{7,6},{8,7},{9,8},{10,9},{11,1... | collective-permute-start | bytes 3145736 | tf_op jit(solution)/shard_map/ppermute | solution.py:15
  235.4 26.0 %collective-permute-start.1 = (f32[1,16,128,128]{3,2,1,0:T(8,128)S(1)}, f32[1,16,128,128]{3,2,1,0:T(8,128)}, u32[]{:S(2)}, u32[]{:S(2)}) collective-permute-start(f32[1,16,128,128]{3,2,1,0:T(8,128)S(1)} %fusion.21), channel_id=1, source_target_pairs={{0,1},{1,2},{2,3},{3,4},{4,5},{5,6},{6,7},{7,8},{8,9},{9,10},{10,1... | collective-permute-start | bytes 3145736 | tf_op jit(solution)/shard_map/ppermute | solution.py:15
  242.0 18.0 %collective-permute-start.6 = (bf16[1,128,512]{2,1,0:T(8,128)(2,1)S(1)}, bf16[1,128,512]{2,1,0:T(8,128)(2,1)S(1)}, u32[]{:S(2)}, u32[]{:S(2)}) collective-permute-start(bf16[1,128,512]{2,1,0:T(8,128)(2,1)S(1)} %copy-done.12), channel_id=1, source_target_pairs={{0,1},{1,2},{2,3},{3,4},{4,5},{5,6},{6,7},{7,8},{8,9},{9,10},{10,1... | collective-permute-start | bytes 393224 | tf_op jit(solution)/shard_map/ppermute | solution.py:15
  264.8 119.7 %copy-start.10 = (bf16[1,128,16,128]{3,2,1,0:T(8,128)(2,1)S(1)}, bf16[1,128,16,128]{3,2,1,0:T(8,128)(2,1)}, u32[]{:S(2)}) copy-start(bf16[1,128,16,128]{3,2,1,0:T(8,128)(2,1)} %param.24) | copy-start | bytes 1572868
  (10 other events, 15.4 us)
Sparse Core Ops, SparseCore 0:
  18.6 86.6 all-gather.2
  216.4 88.7 all-gather.4
